TPU v7x, 32 devices: a whole 2x2x4 slice. The times are simulated.
32 devices in a mesh: dp: 4 (over z), row: 4 (over x, core), col: 2 (over y).
Axes of the slice: x: 2, y: 2, z: 4, core: 2. Of those that a mesh axis runs over, the one named last changes fastest.
Arguments:
- tokens: bfloat16 [11664, 1152], P(('dp', 'col'), 'row'), may hold values from -6 to 6
- ln_gain: bfloat16 [2, 1152], P(None, 'row'), may hold values from 0.5 to 1.5
- ln_bias: bfloat16 [2, 1152], P(None, 'row'), may hold values from -3 to 3
- w_qkv: bfloat16 [1152, 3, 1152], P('row', None, 'col'), may hold values from -0.1875 to 0.1875
- b_qv: bfloat16 [2, 1152], P(None, 'col'), may hold values from -3 to 3
- w_out: bfloat16 [1152, 1152], P('col', 'row'), may hold values from -3 to 3
- b_out: bfloat16 [1152], P('row'), may hold values from -3 to 3
- w_up: bfloat16 [1152, 4304], P('row', 'col'), may hold values from -0.1875 to 0.1875
- b_up: bfloat16 [4304], P('col'), may hold values from -3 to 3
- w_down: bfloat16 [4304, 1152], P('col', 'row'), may hold values from -0.09375 to 0.09375
- b_down: bfloat16 [1152], P('row'), may hold values from -3 to 3
- cotangent: bfloat16 [11664, 1152], P(('dp', 'col'), 'row'), may hold values from -6 to 6
Outputs:
- output: bfloat16 [11664, 1152], P(('dp', 'col'), 'row')
- input_grad: bfloat16 [11664, 1152], P(('dp', 'col'), 'row')
- d_ln_gain: float32 [2, 1152], P(None, 'row')
- d_ln_bias: float32 [2, 1152], P(None, 'row')
- d_w_qkv: float32 [1152, 3, 1152], P(('row', 'dp'), None, 'col')
- d_b_qv: float32 [2, 1152], P(None, 'col')
- d_w_out: float32 [1152, 1152], P(('col', 'dp'), 'row')
- d_b_out: float32 [1152], P('row')
- d_w_up: float32 [1152, 4304], P(('row', 'dp'), 'col')
- d_b_up: float32 [4304], P('col')
- d_w_down: float32 [4304, 1152], P('col', ('row', 'dp'))
- d_b_down: float32 [1152], P('row')
All inputs are finite; a program needn't handle non-finite values.
Results may differ from a plain program's by a relative error of at most 0.018.
Values may be sent and summed in bfloat16 or wider, within the bound.
A program may use at most 192 MiB of HBM per device.

v0:
```python
import jax
import jax.numpy as jnp
from jax import lax
from jax.sharding import PartitionSpec as P

HD = 72
SEQ = 729
epsilon = 1e-06


def gelu_tanh(values):
    return (
        0.5
        * values
        * (1.0 + jnp.tanh(0.7978845608028654 * (values + 0.044715 * values * values * values)))
    )


def row_sums(first_part, second_part):
    return lax.psum((first_part, second_part), "row")


def norm_forward(values, gain, shift):
    full_width = values.shape[1] * lax.axis_size("row")
    row_total, square_total = row_sums(jnp.sum(values, axis=1), jnp.sum(values * values, axis=1))
    row_mean = row_total / full_width
    norm_scale = lax.rsqrt(square_total / full_width - row_mean * row_mean + epsilon)
    normed = (values - row_mean[:, None]) * norm_scale[:, None]
    return (normed, norm_scale, normed * gain + shift)


def norm_backward(incoming, normed, norm_scale, gain):
    full_width = normed.shape[1] * lax.axis_size("row")
    scaled = incoming * gain
    scaled_total, cross_total = row_sums(jnp.sum(scaled, axis=1), jnp.sum(scaled * normed, axis=1))
    back_grad = norm_scale[:, None] * (
        scaled - scaled_total[:, None] / full_width - normed * (cross_total[:, None] / full_width)
    )
    return (back_grad, jnp.sum(incoming * normed, axis=0), jnp.sum(incoming, axis=0))


def gather_tokens(pieces):
    return lax.all_gather(pieces, "col", axis=0, tiled=True)


def sum_over_col(row_term, total_rows):
    return lax.psum_scatter(
        row_term(jnp.int32(0), lax.axis_size("col") * (total_rows // lax.axis_size("col"))),
        "col",
        scatter_dimension=0,
        tiled=True,
    )


def project_in(normed_low, weight):
    rows_all = gather_tokens(normed_low)

    def row_term(first_row, row_count):
        return jnp.dot(rows_all, weight, preferred_element_type=jnp.float32)

    result = lax.psum_scatter(
        row_term(jnp.int32(0), lax.axis_size("row") * (rows_all.shape[0] // lax.axis_size("row"))),
        "row",
        scatter_dimension=0,
        tiled=True,
    )
    return (result, rows_all)


def project_in_back(grad_low, saved_in, weight):
    grads_all = lax.all_gather(grad_low, "row", axis=0, tiled=True)
    weight_grad = lax.dot_general(
        saved_in, grads_all, (((0,), (0,)), ((), ())), preferred_element_type=jnp.float32
    )

    def row_term(first_row, row_count):
        return lax.dot_general(
            grads_all, weight, (((1,), (1,)), ((), ())), preferred_element_type=jnp.float32
        )

    input_grad = sum_over_col(row_term, grads_all.shape[0])
    return (input_grad, weight_grad)


def project_out(inner_low, weight):
    inner_all = lax.all_gather(inner_low, "row", axis=0, tiled=True)

    def row_term(first_row, row_count):
        return jnp.dot(inner_all, weight, preferred_element_type=jnp.float32)

    result = lax.psum_scatter(
        row_term(
            jnp.int32(0), inner_all.shape[0] // lax.axis_size("col") * lax.axis_size("col")
        ).astype(jnp.bfloat16),
        "col",
        scatter_dimension=0,
        tiled=True,
    ).astype(jnp.float32)
    return (result, inner_all)


def project_out_back(grad_low, inner_all, weight):
    grads_all = gather_tokens(grad_low)
    weight_grad = lax.dot_general(
        inner_all, grads_all, (((0,), (0,)), ((), ())), preferred_element_type=jnp.float32
    )
    bias_grad = jnp.sum(grad_low, axis=0, dtype=jnp.float32)

    def row_term(first_row, row_count):
        return lax.dot_general(
            grads_all, weight, (((1,), (1,)), ((), ())), preferred_element_type=jnp.float32
        )

    inner_grad = lax.psum_scatter(
        row_term(jnp.int32(0), lax.axis_size("row") * (grads_all.shape[0] // lax.axis_size("row"))),
        "row",
        scatter_dimension=0,
        tiled=True,
    )
    return (inner_grad, weight_grad, bias_grad)


def attend_forward(image_block):
    queries = image_block[:, 0]
    keys_in = image_block[:, 1]
    values = image_block[:, 2]
    scores = jnp.einsum(
        "qhd,khd->hqk", queries, keys_in, preferred_element_type=jnp.float32
    ) * HD ** (-0.5)
    row_top = jnp.max(scores, axis=-1, keepdims=True)
    exponent = jnp.exp(scores - row_top)
    row_total = jnp.sum(exponent, axis=-1, keepdims=True)
    weights = (exponent / row_total).astype(jnp.bfloat16)
    heads_out = jnp.einsum("hqk,khd->qhd", weights, values, preferred_element_type=jnp.float32)
    return (heads_out.astype(jnp.bfloat16), (row_top + jnp.log(row_total))[..., 0])


def attend_backward(image_block, logsum, grad_heads):
    queries = image_block[:, 0]
    keys_in = image_block[:, 1]
    values = image_block[:, 2]
    scores = jnp.einsum(
        "qhd,khd->hqk", queries, keys_in, preferred_element_type=jnp.float32
    ) * HD ** (-0.5)
    soft_probs = jnp.exp(scores - logsum[..., None])
    weights = soft_probs.astype(jnp.bfloat16)
    value_grad = jnp.einsum("hqk,qhd->khd", weights, grad_heads, preferred_element_type=jnp.float32)
    prob_grad = jnp.einsum("qhd,khd->hqk", grad_heads, values, preferred_element_type=jnp.float32)
    row_delta = jnp.sum(soft_probs * prob_grad, axis=-1, keepdims=True)
    score_grad = (soft_probs * (prob_grad - row_delta)).astype(jnp.bfloat16)
    query_grad = jnp.einsum(
        "hqk,khd->qhd", score_grad, keys_in, preferred_element_type=jnp.float32
    ) * HD ** (-0.5)
    key_grad = jnp.einsum(
        "hqk,qhd->khd", score_grad, queries, preferred_element_type=jnp.float32
    ) * HD ** (-0.5)
    return jnp.stack([query_grad, key_grad, value_grad], axis=1).astype(jnp.bfloat16)


def place_block(block, position, part_count):
    block_size = block.shape[-1]
    zero_vector = jnp.zeros(block.shape[:-1] + (block_size * part_count,), jnp.float32)
    return lax.dynamic_update_slice_in_dim(
        zero_vector, block, position * block_size, block.ndim - 1
    )


def take_block(whole_vector, position, block_size):
    return lax.dynamic_slice_in_dim(
        whole_vector, position * block_size, block_size, whole_vector.ndim - 1
    )


def shards(
    tokens, ln_gain, ln_bias, w_qkv, b_qv, w_out, b_out, w_up, b_up, w_down, b_down, cotangent
):
    inputs = tokens.astype(jnp.float32)
    gain_rows = ln_gain.astype(jnp.float32)
    shift_rows = ln_bias.astype(jnp.float32)
    row_width = tokens.shape[1]
    head_width = b_qv.shape[1]
    heads_here = head_width // HD
    qkv_weight = w_qkv.reshape(row_width, 3 * head_width)
    normed_one, scale_one, first_out = norm_forward(inputs, gain_rows[0], shift_rows[0])
    projected, saved_one = project_in(first_out.astype(jnp.bfloat16), qkv_weight)
    qv_bias = b_qv.astype(jnp.float32)
    bias_rows = jnp.stack([qv_bias[0], jnp.zeros_like(qv_bias[0]), qv_bias[1]])
    images = projected.shape[0] // SEQ
    triple = (projected.reshape(-1, 3, head_width) + bias_rows).astype(jnp.bfloat16)
    triple = triple.reshape(images, SEQ, 3, heads_here, HD)
    heads_low, logsum = lax.map(attend_forward, triple)
    heads_low = heads_low.reshape(-1, head_width)
    attn_part, heads_all = project_out(heads_low, w_out)
    residual = inputs + attn_part + b_out.astype(jnp.float32)
    normed_two, scale_two, second_out = norm_forward(residual, gain_rows[1], shift_rows[1])
    up_total, saved_two = project_in(second_out.astype(jnp.bfloat16), w_up)
    up_value = up_total + b_up.astype(jnp.float32)
    hidden_act, gelu_pull = jax.vjp(gelu_tanh, up_value)
    down_part, hidden_all = project_out(hidden_act.astype(jnp.bfloat16), w_down)
    output = (residual + down_part + b_down.astype(jnp.float32)).astype(jnp.bfloat16)
    act_grad, down_grad, down_bias_grad = project_out_back(cotangent, hidden_all, w_down)
    up_grad = gelu_pull(act_grad)[0].astype(jnp.bfloat16)
    up_bias_grad = jnp.sum(up_grad, axis=0, dtype=jnp.float32)
    second_grad, up_weight_grad = project_in_back(up_grad, saved_two, w_up)
    back_two, gain_two, shift_two = norm_backward(second_grad, normed_two, scale_two, gain_rows[1])
    residual_grad = cotangent.astype(jnp.float32) + back_two
    heads_grad, out_grad, out_bias_grad = project_out_back(
        residual_grad.astype(jnp.bfloat16), heads_all, w_out
    )
    heads_grad = heads_grad.astype(jnp.bfloat16).reshape(images, SEQ, heads_here, HD)
    triple_grad = lax.map(
        lambda image_set: attend_backward(image_set[0], image_set[1], image_set[2]),
        (triple, logsum, heads_grad),
    )
    triple_grad = triple_grad.reshape(-1, 3 * head_width)
    triple_bias_grad = jnp.sum(triple_grad.reshape(-1, 3, head_width), axis=0, dtype=jnp.float32)
    first_grad, triple_weight_grad = project_in_back(triple_grad, saved_one, qkv_weight)
    back_one, gain_one, shift_one = norm_backward(first_grad, normed_one, scale_one, gain_rows[0])
    input_grad = (residual_grad + back_one).astype(jnp.bfloat16)
    row_here = lax.axis_index("row")
    col_here = lax.axis_index("col")
    row_block = jnp.stack([gain_one, gain_two, shift_one, shift_two, out_bias_grad, down_bias_grad])
    row_full = place_block(row_block, row_here, lax.axis_size("row"))
    qv_full = place_block(triple_bias_grad[::2], col_here, lax.axis_size("col"))
    up_full = place_block(up_bias_grad, col_here, lax.axis_size("col"))
    row_summed, qv_summed, up_summed = lax.psum((row_full, qv_full, up_full), ("dp", "row", "col"))
    row_vectors = take_block(row_summed, row_here, row_width)
    qv_vectors = take_block(qv_summed, col_here, head_width)
    up_vector = take_block(up_summed, col_here, up_bias_grad.shape[0])
    triple_shaped = triple_weight_grad.reshape(row_width, 3, head_width)
    triple_total, out_total, up_weight_total, down_total = (
        lax.psum_scatter(
            triple_shaped.astype(jnp.bfloat16), "dp", scatter_dimension=0, tiled=True
        ).astype(jnp.float32),
        lax.psum_scatter(
            out_grad.astype(jnp.bfloat16), "dp", scatter_dimension=0, tiled=True
        ).astype(jnp.float32),
        lax.psum_scatter(
            up_weight_grad.astype(jnp.bfloat16), "dp", scatter_dimension=0, tiled=True
        ).astype(jnp.float32),
        lax.psum_scatter(
            down_grad.astype(jnp.bfloat16), "dp", scatter_dimension=1, tiled=True
        ).astype(jnp.float32),
    )
    return (
        output,
        input_grad,
        row_vectors[0:2],
        row_vectors[2:4],
        triple_total,
        qv_vectors,
        out_total,
        row_vectors[4],
        up_weight_total,
        up_vector,
        down_total,
        row_vectors[5],
    )


def solution(mesh):
    placed = (
        P(("dp", "col"), "row"),
        P(None, "row"),
        P(None, "row"),
        P("row", None, "col"),
        P(None, "col"),
        P("col", "row"),
        P("row"),
        P("row", "col"),
        P("col"),
        P("col", "row"),
        P("row"),
        P(("dp", "col"), "row"),
    )
    return jax.shard_map(
        shards,
        mesh=mesh,
        in_specs=placed,
        out_specs=(
            P(("dp", "col"), "row"),
            P(("dp", "col"), "row"),
            P(None, "row"),
            P(None, "row"),
            P(("row", "dp"), None, "col"),
            P(None, "col"),
            P(("col", "dp"), "row"),
            P("row"),
            P(("row", "dp"), "col"),
            P("col"),
            P("col", ("row", "dp")),
            P("row"),
        ),
        check_vma=False,
    )
```

profile of v0, /device:TPU:0, one launch (start us, length us, event | category | flops | bytes accessed | tf_op | source)
XLA Modules:
  0.0 1888.4 jit_solution(2578188602203052811)
XLA Ops:
  27.7 28.1 %all-gather.17.cloned.1.call-done = bf16[2,1458,288]{1,2,0:T(8,128)(2,1)} async-done(((bf16[1,1458,288]{1,2,0:T(8,128)(2,1)}), bf16[2,1458,288]{1,2,0:T(8,128)(2,1)}) %all-gather.17.cloned.1.call-update) | async-done | bytes 1679632 | tf_op jit(solution)/shard_map/all_gather | solution.py:43
  76.9 181.4 %fusion = f32[736,1728]{1,0:T(8,128)} fusion(f32[2916,1728]{1,0:T(8,128)} %fusion.47), kind=kCustom, calls=%all-reduce-scatter | all-reduce-scatter fusion | flops 5087233 | bytes 25243136
  262.4 14.1 concatenate.2
  317.7 32.9 %all-gather.19.cloned.1.call-done = bf16[4,729,576]{1,2,0:T(8,128)(2,1)} async-done(((bf16[1,729,576]{1,2,0:T(8,128)(2,1)}), bf16[4,729,576]{1,2,0:T(8,128)(2,1)}) %all-gather.19.cloned.1.call-update) | async-done | bytes 3359248 | tf_op jit(solution)/shard_map/all_gather | solution.py:86
  401.2 36.7 %all-reduce.26.cloned.1.call-done = bf16[2916,288]{0,1:T(8,128)(2,1)} async-done(((bf16[2916,288]{0,1:T(8,128)(2,1)}), bf16[2916,288]{0,1:T(8,128)(2,1)}) %all-reduce.26.cloned.1.call-update) | async-done | bytes 1679632
  454.0 218.1 %fusion.2 = f32[736,2152]{1,0:T(8,128)} fusion(f32[2916,2152]{1,0:T(8,128)} %fusion.49), kind=kCustom, calls=%all-reduce-scatter.2 | all-reduce-scatter fusion | flops 6335489 | bytes 31436928
  697.7 219.8 %fusion.1 = f32[736,2152]{1,0:T(8,128)} fusion(f32[2916,2152]{1,0:T(8,128)} %fusion.48), kind=kCustom, calls=%all-reduce-scatter.1 | all-reduce-scatter fusion | flops 6335489 | bytes 31436928
  919.8 17.6 concatenate.4
  937.4 17.6 concatenate.3
  968.0 82.1 %all-gather.27.cloned.1.call-done = bf16[4,729,2152]{2,1,0:T(8,128)(2,1)} async-done(((bf16[1,729,2152]{2,1,0:T(8,128)(2,1)}), bf16[4,729,2152]{2,1,0:T(8,128)(2,1)}) %all-gather.27.cloned.1.call-update) | async-done | bytes 12550480 | tf_op jit(solution)/shard_map/all_gather | solution.py:71
  1050.1 18.0 reshape.103
  1079.0 56.0 %all-gather.23.cloned.1.call-done = bf16[4,729,2152]{2,1,0:T(8,128)(2,1)} async-done(((bf16[1,729,2152]{2,1,0:T(8,128)(2,1)}), bf16[4,729,2152]{2,1,0:T(8,128)(2,1)}) %all-gather.23.cloned.1.call-update) | async-done | bytes 12550480 | tf_op jit(solution)/shard_map/all_gather | solution.py:86
  1135.0 17.4 reshape.99
  1166.2 62.4 %all-reduce.30.cloned.1.call-done = f32[2916,288]{0,1:T(8,128)} async-done(((f32[2916,288]{0,1:T(8,128)}), f32[2916,288]{0,1:T(8,128)}) %all-reduce.30.cloned.1.call-update) | async-done | bytes 3359248
  1243.3 41.8 %all-reduce.28.cloned.1.call-done = bf16[2916,288]{0,1:T(8,128)(2,1)} async-done(((bf16[2916,288]{0,1:T(8,128)(2,1)}), bf16[2916,288]{0,1:T(8,128)(2,1)}) %all-reduce.28.cloned.1.call-update) | async-done | bytes 1679632
  1293.5 28.9 %all-gather.29.cloned.1.call-done = bf16[2,1458,288]{1,2,0:T(8,128)(2,1)} async-done(((bf16[1,1458,288]{1,2,0:T(8,128)(2,1)}), bf16[2,1458,288]{1,2,0:T(8,128)(2,1)}) %all-gather.29.cloned.1.call-update) | async-done | bytes 1679632 | tf_op jit(solution)/shard_map/all_gather | solution.py:43
  1338.5 120.7 %all-reduce.35 = bf16[2916,576]{0,1:T(8,128)(2,1)} all-reduce(f32[2916,576]{0,1:T(8,128)} %fusion.51), channel_id=8, replica_groups=mesh['dp'=4,'row'=4,'col'=2] {'row'}, use_global_device_ids=true, to_apply=%region_20.21.clone | all-reduce | flops 1679616 | bytes 10077696
  1532.8 42.1 %all-gather.31.cloned.1.call-done = bf16[4,729,1728]{2,1,0:T(8,128)(2,1)} async-done(((bf16[1,729,1728]{2,1,0:T(8,128)(2,1)}), bf16[4,729,1728]{2,1,0:T(8,128)(2,1)}) %all-gather.31.cloned.1.call-update) | async-done | bytes 10077712 | tf_op jit(solution)/shard_map/all_gather | solution.py:71
  1574.9 14.8 reshape.107
  1619.4 19.5 %reduce-scatter.23.cloned.1.call-done = bf16[2152,72]{0,1:T(8,128)(2,1)} async-done(((bf16[2152,288]{0,1:T(8,128)(2,1)}), bf16[2152,72]{0,1:T(8,128)(2,1)}) %reduce-scatter.23.cloned.1.call-update) | async-done | bytes 309904
  1642.8 19.0 %reduce-scatter.19.cloned.1.call-done = bf16[144,288]{1,0:T(8,128)(2,1)} async-done(((bf16[576,288]{1,0:T(8,128)(2,1)}), bf16[144,288]{1,0:T(8,128)(2,1)}) %reduce-scatter.19.cloned.1.call-update) | async-done | bytes 82960 | tf_op jit(solution)/shard_map/reduce_scatter | solution.py:235
  1663.4 64.7 %all-reduce.34.cloned.1.call-done = bf16[288,3,576]{2,1,0:T(4,128)(2,1)} async-done(((bf16[288,3,576]{2,1,0:T(4,128)(2,1)}), bf16[288,3,576]{2,1,0:T(4,128)(2,1)}) %all-reduce.34.cloned.1.call-update) | async-done | bytes 995344
  1730.0 90.7 %all-reduce.32.cloned.1.call-done = f32[2916,288]{0,1:T(8,128)} async-done(((f32[2916,288]{0,1:T(8,128)}), f32[2916,288]{0,1:T(8,128)}) %all-reduce.32.cloned.1.call-update) | async-done | bytes 3359248
  1823.7 40.5 %all-reduce.14 = (f32[6,1152]{1,0:T(8,128)S(1)}, f32[2,1152]{1,0:T(2,128)S(1)}, f32[4304]{0:T(1024)S(1)}) all-reduce(f32[6,1152]{1,0:T(8,128)S(1)} %dynamic_update_slice.18, f32[2,1152]{1,0:T(2,128)S(1)} %dynamic_update_slice.19, f32[4304]{0:T(1024)S(1)} %dynamic_update_slice.20), channel_id=1, replica_groups=mesh['dp'=4,'row'=4,'col'=2] {'dp','row','col'}, use_global_device_ids=true, to_apply=%region_33.34 | all-reduce | flops 13520 | bytes 108160 | tf_op jit(solution)/shard_map/psum | solution.py:226
  (191 shorter events, 386.1 us)
Async XLA Ops:
  7.2 677.2 %copy-start = (bf16[288,2152]{1,0:T(8,128)(2,1)S(1)}, bf16[288,2152]{1,0:T(8,128)(2,1)}, u32[]{:S(2)}) copy-start(bf16[288,2152]{1,0:T(8,128)(2,1)} %param.19) | copy-start | bytes 3718660
  7.2 48.7 %all-gather.17.cloned.1.call-start = ((), (), s32[]{:S(2)}) async-start(), calls=%async_computation.4 | async-start | bytes 2654208 | tf_op jit(solution)/shard_map/all_gather | solution.py:43
  26.0 324.6 %all-gather.19.cloned.1.call-start = ((), (), s32[]{:S(2)}) async-start(), calls=%async_computation.5 | async-start | bytes 4423680 | tf_op jit(solution)/shard_map/all_gather | solution.py:86
  76.9 184.3 %copy-start.20 = (u32[32]{0:T(128)S(1)}, u32[32]{0:T(128)}, u32[]{:S(2)}) copy-start(u32[32]{0:T(128)} %constant.88) | copy-start | bytes 388
  259.2 3.2 collective-permute-start
  316.9 64.7 %all-gather.25.cloned.1.call-start = ((), (), s32[]{:S(2)}) async-start(), calls=%async_computation.8 | async-start | bytes 2654208 | tf_op jit(solution)/shard_map/all_gather | solution.py:43
  317.6 120.3 %all-reduce.26.cloned.1.call-start = ((), (), s32[]{:S(2)}) async-start(), calls=%async_computation.12 | async-start | bytes 3391488
  369.7 304.9 %all-gather.21.cloned.1.call-start = ((), (), s32[]{:S(2)}) async-start(), calls=%async_computation.6 | async-start | bytes 2654208 | tf_op jit(solution)/shard_map/all_gather | solution.py:43
  453.9 596.1 %all-gather.27.cloned.1.call-start = ((), (), s32[]{:S(2)}) async-start(), calls=%async_computation.9 | async-start | bytes 16015360 | tf_op jit(solution)/shard_map/all_gather | solution.py:71
  673.0 246.8 %collective-permute-start.2 = (f32[21,2152]{1,0:T(8,128)S(1)}, f32[21,2152]{1,0:T(8,128)S(1)}, u32[]{:S(2)}, u32[]{:S(2)}) collective-permute-start(f32[21,2152]{1,0:T(8,128)S(1)} %slice.78), channel_id=1, source_target_pairs={{0,2},{2,4},{4,6},{1,3},{3,5},{5,7},{8,10},{10,12},{12,14},{9,11},... | collective-permute-start | bytes 542312
  697.7 222.1 %copy-start.19 = (bf16[2152]{0:T(1024)(128)(2,1)S(1)}, bf16[2152]{0:T(1024)(128)(2,1)}, u32[]{:S(2)}) copy-start(bf16[2152]{0:T(1024)(128)(2,1)} %param.20) | copy-start | bytes 12916
  918.5 19.0 %collective-permute-start.1 = (f32[21,2152]{1,0:T(8,128)S(1)}, f32[21,2152]{1,0:T(8,128)S(1)}, u32[]{:S(2)}, u32[]{:S(2)}) collective-permute-start(f32[21,2152]{1,0:T(8,128)S(1)} %slice.77), channel_id=1, source_target_pairs={{0,2},{2,4},{4,6},{1,3},{3,5},{5,7},{8,10},{10,12},{12,14},{9,11},... | collective-permute-start | bytes 542312
  966.8 168.3 %all-gather.23.cloned.1.call-start = ((), (), s32[]{:S(2)}) async-start(), calls=%async_computation.7 | async-start | bytes 16015360 | tf_op jit(solution)/shard_map/all_gather | solution.py:86
  967.5 261.1 %all-reduce.30.cloned.1.call-start = ((), (), s32[]{:S(2)}) async-start(), calls=%async_computation.14 | async-start | bytes 6782976
  1078.8 206.3 %all-reduce.28.cloned.1.call-start = ((), (), s32[]{:S(2)}) async-start(), calls=%async_computation.13 | async-start | bytes 3391488
  1166.1 156.3 %all-gather.29.cloned.1.call-start = ((), (), s32[]{:S(2)}) async-start(), calls=%async_computation.10 | async-start | bytes 2654208 | tf_op jit(solution)/shard_map/all_gather | solution.py:43
  1292.8 282.1 %all-gather.31.cloned.1.call-start = ((), (), s32[]{:S(2)}) async-start(), calls=%async_computation.11 | async-start | bytes 13189120 | tf_op jit(solution)/shard_map/all_gather | solution.py:71
  1504.7 112.9 %reduce-scatter.21.cloned.1.call-start = ((), (), s32[]{:S(2)}) async-start(), calls=%async_computation.17 | async-start | bytes 1566720
  1515.4 123.5 %reduce-scatter.23.cloned.1.call-start = ((), (), s32[]{:S(2)}) async-start(), calls=%async_computation.18 | async-start | bytes 1566720
  1527.3 134.5 %reduce-scatter.19.cloned.1.call-start = ((), (), s32[]{:S(2)}) async-start(), calls=%async_computation.3 | async-start | bytes 552960 | tf_op jit(solution)/shard_map/reduce_scatter | solution.py:235
  1532.6 195.5 %all-reduce.34.cloned.1.call-start = ((), (), s32[]{:S(2)}) async-start(), calls=%async_computation.16 | async-start | bytes 2949120
  1605.5 215.2 %all-reduce.32.cloned.1.call-start = ((), (), s32[]{:S(2)}) async-start(), calls=%async_computation.15 | async-start | bytes 6782976
  1640.8 180.0 %copy-start.13 = (f32[1458]{0:T(1024)S(1)}, f32[1458]{0:T(1024)}, u32[]{:S(2)}) copy-start(f32[1458]{0:T(1024)} %copy-done.12) | copy-start | bytes 17500
  1640.8 180.0 %copy-start.15 = (f32[1458]{0:T(1024)S(1)}, f32[1458]{0:T(1024)}, u32[]{:S(2)}) copy-start(f32[1458]{0:T(1024)} %copy-done.14) | copy-start | bytes 17500
  (20 other events, 535.5 us)
Sparse Core Ops, SparseCore 0:
  26.1 29.7 all-gather.16
  317.0 33.4 all-gather.18
  352.1 29.3 all-gather.24
  383.7 54.1 all-reduce.25
  454.1 29.0 all-gather.20
  966.9 83.1 all-gather.26
  1051.6 83.3 all-gather.22
  1137.4 91.1 all-reduce.29
  1230.9 54.1 all-reduce.27
  1292.9 29.4 all-gather.28
  1504.8 70.0 all-gather.30
  1577.1 30.2 reduce-scatter.20
  1609.7 29.1 reduce-scatter.22
  1641.6 20.1 reduce-scatter.18
  1664.0 64.0 all-reduce.33
  1730.3 90.4 all-reduce.31
where the time goes:
time: 1900 us; the launch traced here: 1890 us
  blocking collectives  826 us (43%)
  waiting for transfers between devices  617 us (32%)
  local copies, waits for them, and re-layouts  186 us (10%)
  matrix products  162 us (9%)
  other arithmetic  73.3 us (4%)
    unnamed x4, blocking collectives  740 us
    unnamed x26, waiting for transfers between devices  317 us
    unnamed x71, local copies, waits for them, and re-layouts  144 us
    all_gather x2, waiting for transfers between devices, project_in_back(): grads_all = lax.all_gather(grad_low, 'row', axis=0, tiled=True)  124 us
    all_gather x2, waiting for transfers between devices, project_out(): inner_all = lax.all_gather(inner_low, 'row', axis=0, tiled=True)  88.9 us
    all_gather x4, waiting for transfers between devices, gather_tokens(): return lax.all_gather(pieces, 'col', axis=0, tiled=True)  67.5 us
    psum x4, blocking collectives, row_sums(): return lax.psum((first_part, second_part), 'row')  45.8 us
    psum x1, blocking collectives, shards(): lax.psum((row_full, qv_full, up_full), ('dp', 'row', 'col'))  40.5 us
  transfers between devices with their start and end apart: 19, of which 14 were waited for; matrix products, arithmetic and copies ran while one was open for 35% of the time, Pallas kernels for 0%

commit v1 on v0

--- a/solution.py
+++ b/solution.py
@@ -6,6 +6,19 @@
 HD = 72
 SEQ = 729
 epsilon = 1e-06
+
+
+def collect(value, axis, dim):
+    ways = lax.axis_size(axis)
+    up = [(d, (d + 1) % ways) for d in range(ways)]
+    down = [(d, (d - 1) % ways) for d in range(ways)]
+    earlier, later = ([value], [value])
+    for _ in range(ways // 2):
+        earlier.append(lax.ppermute(earlier[-1], axis, up))
+    for _ in range((ways - 1) // 2):
+        later.append(lax.ppermute(later[-1], axis, down))
+    line = jnp.concatenate([*earlier[::-1], *later[1:]], axis=dim)
+    return jnp.roll(line, (lax.axis_index(axis) - ways // 2) * value.shape[dim], axis=dim)
 
 
 def gelu_tanh(values):
@@ -68,7 +81,7 @@
 
 
 def project_in_back(grad_low, saved_in, weight):
-    grads_all = lax.all_gather(grad_low, "row", axis=0, tiled=True)
+    grads_all = collect(grad_low, "row", 0)
     weight_grad = lax.dot_general(
         saved_in, grads_all, (((0,), (0,)), ((), ())), preferred_element_type=jnp.float32
     )

time: 1900 us -> 2090 us (1.10)
  local copies, waits for them, and re-layouts: 186 us -> 380 us
    ppermute x0 -> x6, waiting for transfers between devices: none -> 233 us  [the longest x4 226 us: collect(): earlier.append(lax.ppermute(earlier[-1], axis, up))]
    concatenate x0 -> x2, local copies, waits for them, and re-layouts: none -> 228 us  [collect(): jnp.roll(line, (lax.axis_index(axis) - ways // 2) * value.shape[dim], axi...]
    all_gather x2 -> x0, waiting for transfers between devices: 124 us -> none  [project_in_back(): grads_all = lax.all_gather(grad_low, 'row', axis=0, tiled=True)]
    all_gather x2, waiting for transfers between devices: 88.9 us -> 33.2 us  [project_out(): inner_all = lax.all_gather(inner_low, 'row', axis=0, tiled=True)]
    unnamed x26 -> x24, waiting for transfers between devices: 317 us -> 276 us
    unnamed x71 -> x70, local copies, waits for them, and re-layouts: 144 us -> 106 us
  transfers between devices with their start and end apart: 19 -> 23, of which waited for: 14 -> 15; matrix products, arithmetic and copies ran while one was open for 35% -> 41% of each run, Pallas kernels for 0% -> 0%
where the time goes in v1:
time: 2090 us; the launch traced here: 2080 us
  blocking collectives  826 us (40%)
  waiting for transfers between devices  609 us (29%)
  local copies, waits for them, and re-layouts  380 us (18%)
  matrix products  161 us (8%)
  other arithmetic  73.8 us (4%)
    unnamed x4, blocking collectives  740 us
    unnamed x24, waiting for transfers between devices  276 us
    concatenate x2, local copies, waits for them, and re-layouts, collect(): jnp.roll(line, (lax.axis_index(axis) - ways // 2) * value.shape[dim], axi...  228 us
    ppermute x4, waiting for transfers between devices, collect(): earlier.append(lax.ppermute(earlier[-1], axis, up))  226 us
    unnamed x70, local copies, waits for them, and re-layouts  106 us
    all_gather x4, waiting for transfers between devices, gather_tokens(): return lax.all_gather(pieces, 'col', axis=0, tiled=True)  67.3 us
    psum x4, blocking collectives, row_sums(): return lax.psum((first_part, second_part), 'row')  46 us
  transfers between devices with their start and end apart: 23, of which 15 were waited for; matrix products, arithmetic and copies ran while one was open for 41% of the time, Pallas kernels for 0%

profile of v1, /device:TPU:0, one launch (start us, length us, event | category | flops | bytes accessed | tf_op | source)
XLA Modules:
  0.0 2077.2 jit_solution(12664725820112297892)
XLA Ops:
  27.8 28.1 %all-gather.13.cloned.1.call-done = bf16[2,1458,288]{1,2,0:T(8,128)(2,1)} async-done(((bf16[1,1458,288]{1,2,0:T(8,128)(2,1)}), bf16[2,1458,288]{1,2,0:T(8,128)(2,1)}) %all-gather.13.cloned.1.call-update) | async-done | bytes 1679632 | tf_op jit(solution)/shard_map/all_gather | solution.py:56
  76.9 181.5 %fusion = f32[736,1728]{1,0:T(8,128)} fusion(f32[2916,1728]{1,0:T(8,128)} %fusion.65), kind=kCustom, calls=%all-reduce-scatter | all-reduce-scatter fusion | flops 5087233 | bytes 25243136
  262.3 14.1 concatenate.16
  317.6 33.1 %all-gather.15.cloned.1.call-done = bf16[4,729,576]{1,2,0:T(8,128)(2,1)} async-done(((bf16[1,729,576]{1,2,0:T(8,128)(2,1)}), bf16[4,729,576]{1,2,0:T(8,128)(2,1)}) %all-gather.15.cloned.1.call-update) | async-done | bytes 3359248 | tf_op jit(solution)/shard_map/all_gather | solution.py:99
  387.5 13.9 fusion.67
  401.5 36.7 %all-reduce.26.cloned.1.call-done = bf16[2916,288]{0,1:T(8,128)(2,1)} async-done(((bf16[2916,288]{0,1:T(8,128)(2,1)}), bf16[2916,288]{0,1:T(8,128)(2,1)}) %all-reduce.26.cloned.1.call-update) | async-done | bytes 1679632
  454.2 218.2 %fusion.2 = f32[736,2152]{1,0:T(8,128)} fusion(f32[2916,2152]{1,0:T(8,128)} %fusion.67), kind=kCustom, calls=%all-reduce-scatter.2 | all-reduce-scatter fusion | flops 6335489 | bytes 31436928
  697.7 219.8 %fusion.1 = f32[736,2152]{1,0:T(8,128)} fusion(f32[2916,2152]{1,0:T(8,128)} %fusion.66), kind=kCustom, calls=%all-reduce-scatter.1 | all-reduce-scatter fusion | flops 6335489 | bytes 31436928
  919.8 17.5 concatenate.18
  937.3 17.6 concatenate.17
  969.1 126.8 %collective-permute-done = bf16[729,2152]{1,0:T(8,128)(2,1)} collective-permute-done((bf16[729,2152]{1,0:T(8,128)(2,1)}, bf16[729,2152]{1,0:T(8,128)(2,1)}, u32[]{:S(2)}, u32[]{:S(2)}) %collective-permute-start) | collective-permute-done | bytes 3137648 | tf_op jit(solution)/shard_map/ppermute | solution.py:17
  1099.2 43.0 %collective-permute-done.1 = bf16[729,2152]{1,0:T(8,128)(2,1)} collective-permute-done((bf16[729,2152]{1,0:T(8,128)(2,1)}, bf16[729,2152]{1,0:T(8,128)(2,1)}, u32[]{:S(2)}, u32[]{:S(2)}) %collective-permute-start.1) | collective-permute-done | bytes 3137648 | tf_op jit(solution)/shard_map/ppermute | solution.py:17
  1142.2 126.4 %concatenate.14 = bf16[5832,2152]{1,0:T(8,128)(2,1)} concatenate(bf16[729,2152]{1,0:T(8,128)(2,1)} %collective-permute-done.1, bf16[729,2152]{1,0:T(8,128)(2,1)} %collective-permute-done, bf16[729,2152]{1,0:T(8,128)(2,1)} %get-tuple-element.93, bf16[729,2152]{1,0:T(8,128)(2,1)} %collective-permute-done.2, bf16[729,2152]{1,0:T(8,128)(2,1)} %collective-permute-done.1, ...), dimensions={0} | concatenate | bytes 50201856 | tf_op jit(solution)/shard_map/jit(_roll_dynamic)/concatenate | solution.py:21
  1279.5 17.0 reshape.99
  1310.2 60.0 %all-reduce.30.cloned.1.call-done = f32[2916,288]{0,1:T(8,128)} async-done(((f32[2916,288]{0,1:T(8,128)}), f32[2916,288]{0,1:T(8,128)}) %all-reduce.30.cloned.1.call-update) | async-done | bytes 3359248
  1385.2 41.6 %all-reduce.28.cloned.1.call-done = bf16[2916,288]{0,1:T(8,128)(2,1)} async-done(((bf16[2916,288]{0,1:T(8,128)(2,1)}), bf16[2916,288]{0,1:T(8,128)(2,1)}) %all-reduce.28.cloned.1.call-update) | async-done | bytes 1679632
  1435.2 28.9 %all-gather.23.cloned.1.call-done = bf16[2,1458,288]{1,2,0:T(8,128)(2,1)} async-done(((bf16[1,1458,288]{1,2,0:T(8,128)(2,1)}), bf16[2,1458,288]{1,2,0:T(8,128)(2,1)}) %all-gather.23.cloned.1.call-update) | async-done | bytes 1679632 | tf_op jit(solution)/shard_map/all_gather | solution.py:56
  1480.2 120.4 %all-reduce.35 = bf16[2916,576]{0,1:T(8,128)(2,1)} all-reduce(f32[2916,576]{0,1:T(8,128)} %fusion.68), channel_id=8, replica_groups=mesh['dp'=4,'row'=4,'col'=2] {'row'}, use_global_device_ids=true, to_apply=%region_20.21.clone | all-reduce | flops 1679616 | bytes 10077696
  1658.8 35.4 %collective-permute-done.3 = bf16[729,1728]{1,0:T(8,128)(2,1)} collective-permute-done((bf16[729,1728]{1,0:T(8,128)(2,1)}, bf16[729,1728]{1,0:T(8,128)(2,1)}, u32[]{:S(2)}, u32[]{:S(2)}) %collective-permute-start.3) | collective-permute-done | bytes 2519456 | tf_op jit(solution)/shard_map/ppermute | solution.py:17
  1713.4 21.0 %collective-permute-done.4 = bf16[729,1728]{1,0:T(8,128)(2,1)} collective-permute-done((bf16[729,1728]{1,0:T(8,128)(2,1)}, bf16[729,1728]{1,0:T(8,128)(2,1)}, u32[]{:S(2)}, u32[]{:S(2)}) %collective-permute-start.4) | collective-permute-done | bytes 2519456 | tf_op jit(solution)/shard_map/ppermute | solution.py:17
  1734.5 101.1 %concatenate.15 = bf16[5832,1728]{1,0:T(8,128)(2,1)} concatenate(bf16[729,1728]{1,0:T(8,128)(2,1)} %collective-permute-done.4, bf16[729,1728]{1,0:T(8,128)(2,1)} %collective-permute-done.3, bf16[729,1728]{1,0:T(8,128)(2,1)} %copy.54, bf16[729,1728]{1,0:T(8,128)(2,1)} %collective-permute-done.5, bf16[729,1728]{1,0:T(8,128)(2,1)} %collective-permute-done.4, ...), dimensions={0} | concatenate | bytes 40310784 | tf_op jit(solution)/shard_map/jit(_roll_dynamic)/concatenate | solution.py:21
  1870.8 46.0 %all-reduce.34.cloned.1.call-done = bf16[288,3,576]{2,1,0:T(4,128)(2,1)} async-done(((bf16[288,3,576]{2,1,0:T(4,128)(2,1)}), bf16[288,3,576]{2,1,0:T(4,128)(2,1)}) %all-reduce.34.cloned.1.call-update) | async-done | bytes 995344
  1918.6 90.7 %all-reduce.32.cloned.1.call-done = f32[2916,288]{0,1:T(8,128)} async-done(((f32[2916,288]{0,1:T(8,128)}), f32[2916,288]{0,1:T(8,128)}) %all-reduce.32.cloned.1.call-update) | async-done | bytes 3359248
  2012.4 40.5 %all-reduce.14 = (f32[6,1152]{1,0:T(8,128)S(1)}, f32[2,1152]{1,0:T(2,128)S(1)}, f32[4304]{0:T(1024)S(1)}) all-reduce(f32[6,1152]{1,0:T(8,128)S(1)} %dynamic_update_slice.18, f32[2,1152]{1,0:T(2,128)S(1)} %dynamic_update_slice.19, f32[4304]{0:T(1024)S(1)} %dynamic_update_slice.20), channel_id=1, replica_groups=mesh['dp'=4,'row'=4,'col'=2] {'dp','row','col'}, use_global_device_ids=true, to_apply=%region_33.34 | all-reduce | flops 13520 | bytes 108160 | tf_op jit(solution)/shard_map/psum | solution.py:239
  (199 shorter events, 380.4 us)
Async XLA Ops:
  7.2 677.4 %copy-start = (bf16[288,2152]{1,0:T(8,128)(2,1)S(1)}, bf16[288,2152]{1,0:T(8,128)(2,1)}, u32[]{:S(2)}) copy-start(bf16[288,2152]{1,0:T(8,128)(2,1)} %param.19) | copy-start | bytes 3718660
  7.2 48.7 %all-gather.13.cloned.1.call-start = ((), (), s32[]{:S(2)}) async-start(), calls=%async_computation.4 | async-start | bytes 2654208 | tf_op jit(solution)/shard_map/all_gather | solution.py:56
  26.0 324.7 %all-gather.15.cloned.1.call-start = ((), (), s32[]{:S(2)}) async-start(), calls=%async_computation.5 | async-start | bytes 4423680 | tf_op jit(solution)/shard_map/all_gather | solution.py:99
  259.4 2.9 collective-permute-start.6
  316.8 64.9 %all-gather.21.cloned.1.call-start = ((), (), s32[]{:S(2)}) async-start(), calls=%async_computation.8 | async-start | bytes 2654208 | tf_op jit(solution)/shard_map/all_gather | solution.py:56
  317.5 120.6 %all-reduce.26.cloned.1.call-start = ((), (), s32[]{:S(2)}) async-start(), calls=%async_computation.10 | async-start | bytes 3391488
  369.7 305.1 %all-gather.17.cloned.1.call-start = ((), (), s32[]{:S(2)}) async-start(), calls=%async_computation.6 | async-start | bytes 2654208 | tf_op jit(solution)/shard_map/all_gather | solution.py:56
  454.1 825.4 %all-gather.19.cloned.1.call-start = ((), (), s32[]{:S(2)}) async-start(), calls=%async_computation.7 | async-start | bytes 16015360 | tf_op jit(solution)/shard_map/all_gather | solution.py:99
  673.3 246.5 %collective-permute-start.8 = (f32[21,2152]{1,0:T(8,128)S(1)}, f32[21,2152]{1,0:T(8,128)S(1)}, u32[]{:S(2)}, u32[]{:S(2)}) collective-permute-start(f32[21,2152]{1,0:T(8,128)S(1)} %slice.78), channel_id=1, source_target_pairs={{0,2},{2,4},{4,6},{1,3},{3,5},{5,7},{8,10},{10,12},{12,14},{9,11},... | collective-permute-start | bytes 542312
  918.5 18.8 collective-permute-start.7
  967.2 403.0 %all-reduce.30.cloned.1.call-start = ((), (), s32[]{:S(2)}) async-start(), calls=%async_computation.12 | async-start | bytes 6782976
  967.3 128.6 %collective-permute-start = (bf16[729,2152]{1,0:T(8,128)(2,1)}, bf16[729,2152]{1,0:T(8,128)(2,1)}, u32[]{:S(2)}, u32[]{:S(2)}) collective-permute-start(bf16[729,2152]{1,0:T(8,128)(2,1)} %get-tuple-element.93), channel_id=1, source_target_pairs={{0,2},{2,4},{4,6},{6,0},{1,3},{3,5},{5,7},{7,1},{8,10},{10,12},{12... | collective-permute-start | bytes 9412856 | tf_op jit(solution)/shard_map/ppermute | solution.py:17
  968.4 130.8 %collective-permute-start.2 = (bf16[729,2152]{1,0:T(8,128)(2,1)}, bf16[729,2152]{1,0:T(8,128)(2,1)}, u32[]{:S(2)}, u32[]{:S(2)}) collective-permute-start(bf16[729,2152]{1,0:T(8,128)(2,1)} %get-tuple-element.93), channel_id=1, source_target_pairs={{0,6},{2,0},{4,2},{6,4},{1,7},{3,1},{5,3},{7,5},{8,14},{10,8},{12,... | collective-permute-start | bytes 9412856 | tf_op jit(solution)/shard_map/ppermute | solution.py:19
  1095.9 46.4 %collective-permute-start.1 = (bf16[729,2152]{1,0:T(8,128)(2,1)}, bf16[729,2152]{1,0:T(8,128)(2,1)}, u32[]{:S(2)}, u32[]{:S(2)}) collective-permute-start(bf16[729,2152]{1,0:T(8,128)(2,1)} %collective-permute-done), channel_id=1, source_target_pairs={{0,2},{2,4},{4,6},{6,0},{1,3},{3,5},{5,7},{7,1},{8,10},{10,12},{12... | collective-permute-start | bytes 9412856 | tf_op jit(solution)/shard_map/ppermute | solution.py:17
  1279.5 147.3 %all-reduce.28.cloned.1.call-start = ((), (), s32[]{:S(2)}) async-start(), calls=%async_computation.11 | async-start | bytes 3391488
  1310.1 154.0 %all-gather.23.cloned.1.call-start = ((), (), s32[]{:S(2)}) async-start(), calls=%async_computation.9 | async-start | bytes 2654208 | tf_op jit(solution)/shard_map/all_gather | solution.py:56
  1434.5 428.9 %reduce-scatter.21.cloned.1.call-start = ((), (), s32[]{:S(2)}) async-start(), calls=%async_computation.15 | async-start | bytes 1566720
  1646.2 48.1 %collective-permute-start.3 = (bf16[729,1728]{1,0:T(8,128)(2,1)}, bf16[729,1728]{1,0:T(8,128)(2,1)}, u32[]{:S(2)}, u32[]{:S(2)}) collective-permute-start(bf16[729,1728]{1,0:T(8,128)(2,1)} %copy.54), channel_id=1, source_target_pairs={{0,2},{2,4},{4,6},{6,0},{1,3},{3,5},{5,7},{7,1},{8,10},{10,12},{12... | collective-permute-start | bytes 7558280 | tf_op jit(solution)/shard_map/ppermute | solution.py:17
  1657.5 207.7 %reduce-scatter.23.cloned.1.call-start = ((), (), s32[]{:S(2)}) async-start(), calls=%async_computation.16 | async-start | bytes 1566720
  1657.6 55.8 %collective-permute-start.5 = (bf16[729,1728]{1,0:T(8,128)(2,1)}, bf16[729,1728]{1,0:T(8,128)(2,1)}, u32[]{:S(2)}, u32[]{:S(2)}) collective-permute-start(bf16[729,1728]{1,0:T(8,128)(2,1)} %copy.54), channel_id=1, source_target_pairs={{0,6},{2,0},{4,2},{6,4},{1,7},{3,1},{5,3},{7,5},{8,14},{10,8},{12,... | collective-permute-start | bytes 7558280 | tf_op jit(solution)/shard_map/ppermute | solution.py:19
  1694.2 40.2 %collective-permute-start.4 = (bf16[729,1728]{1,0:T(8,128)(2,1)}, bf16[729,1728]{1,0:T(8,128)(2,1)}, u32[]{:S(2)}, u32[]{:S(2)}) collective-permute-start(bf16[729,1728]{1,0:T(8,128)(2,1)} %collective-permute-done.3), channel_id=1, source_target_pairs={{0,2},{2,4},{4,6},{6,0},{1,3},{3,5},{5,7},{7,1},{8,10},{10,12},{12... | collective-permute-start | bytes 7558280 | tf_op jit(solution)/shard_map/ppermute | solution.py:17
  1704.7 164.5 %reduce-scatter.19.cloned.1.call-start = ((), (), s32[]{:S(2)}) async-start(), calls=%async_computation.3 | async-start | bytes 552960 | tf_op jit(solution)/shard_map/reduce_scatter | solution.py:248
  1709.9 206.8 %all-reduce.34.cloned.1.call-start = ((), (), s32[]{:S(2)}) async-start(), calls=%async_computation.14 | async-start | bytes 2949120
  1851.4 158.0 %all-reduce.32.cloned.1.call-start = ((), (), s32[]{:S(2)}) async-start(), calls=%async_computation.13 | async-start | bytes 6782976
  (25 other events, 1198.3 us)
Sparse Core Ops, SparseCore 0:
  26.1 29.7 all-gather.12
  316.9 33.7 all-gather.14
  352.3 29.3 all-gather.20
  383.9 54.1 all-reduce.25
  454.2 29.0 all-gather.16
  967.4 146.6 all-gather.18
  1279.6 90.5 all-reduce.29
  1372.5 54.1 all-reduce.27
  1434.6 29.4 all-gather.22
  1657.7 29.9 reduce-scatter.20
  1704.8 30.5 reduce-scatter.22
  1738.1 20.1 reduce-scatter.18
  1851.5 65.1 all-reduce.33
  1918.9 90.4 all-reduce.31
